TPU v7x, 512 devices: a whole 4x8x8 slice. The times are simulated.
512 devices in a mesh: nest: 8 (over x, z_hi), gx: 8 (over y), gy: 8 (over z_lo, core).
Axes of the slice: x: 4, y: 8, z: 8 (z_hi: 2, z_lo: 4; z = z_hi * 4 + z_lo), core: 2. Of those that a mesh axis runs over, the one named last changes fastest.
Arguments:
- state: float32 [8, 4, 8, 128, 1024], P('nest', None, None, 'gx', 'gy'), may hold values from -6 to 6
- metric: float32 [8, 3, 128, 1024], P('nest', None, 'gx', 'gy'), may hold values from -1.2 to 1.4, as said below
- placement: int32 [7, 2], replicated, may hold values from 0 to 682, as said below
- zones: int32 [7, 4], replicated, may hold values from 2 to 5
Outputs:
- new_state: float32 [8, 4, 8, 128, 1024], P('nest', None, None, 'gx', 'gy')
Inputs may be any that keep to these rules, and one draw needn't show every extreme that they name: metric[:, 0] and metric[:, 1] are terrain slopes; metric[:, 2] is the column stretch, between 0.6 and 1.4. placement[n] = (ox, oy) with ox <= 85 and oy <= 682.
All inputs are finite; a program needn't handle non-finite values.
Results may differ from a plain program's by a relative error of at most 0.0003.
Values sent between devices are 32-bit elements; how exact they have to be, the bound alone decides.
No kernel may reach another device: no remote copies, remote signals or barrier semaphores. Data moves between devices by JAX's collectives and lax.ppermute only.
A program may use at most 64 MiB of HBM per device.

v0:
```python
import jax
import jax.numpy as jnp
from jax import lax
from jax.sharding import PartitionSpec as P

SUB = 4
R = 3
W_MAX = 5
WP = 3
TIME_STEP = 0.5
SOUND_SQ = 1.0
PRECISE = lax.Precision.HIGHEST


def extended(value, sides, width):
    for axis, dim in sides:
        devices, length = (lax.axis_size(axis), value.shape[dim])
        up = [(i, (i + 1) % devices) for i in range(devices - 1)]
        down = [(j, i) for i, j in up]
        last = lax.slice_in_dim(value, length - width, length, axis=dim)
        initial = lax.slice_in_dim(value, 0, width, axis=dim)
        before = lax.ppermute(last, axis, up)
        after = lax.ppermute(initial, axis, down)
        value = jnp.concatenate([before, value, after], axis=dim)
    return value


def broadcast(block, axis, owner):
    block = jnp.where(lax.axis_index(axis) == owner, block, jnp.zeros_like(block))
    return lax.psum(block, axis)


def vertical(field):
    upper = jnp.concatenate([field[1:], field[-1:]], 0)
    lower = jnp.concatenate([field[:1], field[:-1]], 0)
    return (upper - lower) * 0.5


def edge_weight(zone_width, row_index, col_index, total_x, total_y):
    widths = zone_width.astype(jnp.float32)
    row_pos = row_index.astype(jnp.float32)[:, None]
    col_pos = col_index.astype(jnp.float32)[None, :]
    dists = (row_pos, total_x - 1 - row_pos, col_pos, total_y - 1 - col_pos)
    weight = jnp.zeros((row_index.shape[0], col_index.shape[0]), jnp.float32)
    for edge in range(4):
        weight = jnp.maximum(weight, jnp.maximum((widths[edge] - dists[edge]) / widths[edge], 0.0))
    return weight


def step_each(current, terrain, sigma_col):
    wind_x, wind_y, updraft, pressure = current
    pressure_ext = extended(pressure, (("gx", 1), ("gy", 2)), 1)
    press_z = vertical(pressure) / terrain[2]
    grad_x = (pressure_ext[:, 2:, 1:-1] - pressure_ext[:, :-2, 1:-1]) * 0.5
    grad_y = (pressure_ext[:, 1:-1, 2:] - pressure_ext[:, 1:-1, :-2]) * 0.5
    new_x = wind_x - TIME_STEP * (grad_x - sigma_col * terrain[0] * press_z)
    new_y = wind_y - TIME_STEP * (grad_y - sigma_col * terrain[1] * press_z)
    new_w = updraft - TIME_STEP * press_z
    winds_ext = extended(jnp.stack([new_x, new_y]), (("gx", 2), ("gy", 3)), 1)
    spread = (winds_ext[0, :, 2:, 1:-1] - winds_ext[0, :, :-2, 1:-1]) * 0.5 + (
        winds_ext[1, :, 1:-1, 2:] - winds_ext[1, :, 1:-1, :-2]
    ) * 0.5
    spread = (
        spread
        - sigma_col * (terrain[0] * vertical(new_x) + terrain[1] * vertical(new_y)) / terrain[2]
        + vertical(new_w) / terrain[2]
    )
    return (new_x, new_y, new_w, pressure - TIME_STEP * SOUND_SQ * spread)


def boundary_pieces(
    parent_tile, placement, row_start, col_start, total_x, total_y, foot_x, foot_y, span_len
):
    row_index = row_start + jnp.arange(parent_tile.shape[2], dtype=jnp.int32)
    col_index = col_start + jnp.arange(parent_tile.shape[3], dtype=jnp.int32)
    depth_range = jnp.arange(WP, dtype=jnp.int32)
    reach_range = jnp.arange(span_len, dtype=jnp.int32)
    west_x = placement[:, 0:1]
    south_y = placement[:, 1:2]
    east_base = (total_x - 1) // R - (WP - 1)
    north_base = (total_y - 1) // R - (WP - 1)
    x_depth = jnp.stack([west_x + depth_range, west_x + east_base + depth_range], 1)
    y_depth = jnp.stack([south_y + depth_range, south_y + north_base + depth_range], 1)
    x_reach = jnp.where(reach_range < foot_x, west_x + reach_range, -1)
    y_reach = jnp.where(reach_range < foot_y, south_y + reach_range, -1)
    pick_rows = (x_depth[..., None] == row_index).astype(jnp.float32)
    pick_cols = (y_reach[:, None, :] == col_index[None, :, None]).astype(jnp.float32)
    across = jnp.einsum("neai,flij->neflaj", pick_rows, parent_tile, precision=PRECISE)
    across = jnp.einsum("neflaj,njb->neflab", across, pick_cols, precision=PRECISE)
    pick_depth = (y_depth[..., None] == col_index).astype(jnp.float32)
    pick_reach = (x_reach[:, None, :] == row_index[None, :, None]).astype(jnp.float32)
    along_y = jnp.einsum("neaj,flij->neflai", pick_depth, parent_tile, precision=PRECISE)
    along_y = jnp.einsum("neflai,nib->neflab", along_y, pick_reach, precision=PRECISE)
    return jnp.concatenate([across, along_y], 1)


def relax_edges(relaxed_in, own_pieces, zone_width, row_start, col_start, total_x, total_y, active):
    row_index = row_start + jnp.arange(relaxed_in.shape[2], dtype=jnp.int32)
    col_index = col_start + jnp.arange(relaxed_in.shape[3], dtype=jnp.int32)
    depth_range = jnp.arange(WP, dtype=jnp.int32)
    reach_range = jnp.arange(own_pieces.shape[-1], dtype=jnp.int32)
    east_base = (total_x - 1) // R - (WP - 1)
    north_base = (total_y - 1) // R - (WP - 1)
    west_pick = ((row_index < W_MAX)[:, None] & ((row_index // R)[:, None] == depth_range)).astype(
        jnp.float32
    )
    east_pick = (
        (row_index >= total_x - W_MAX)[:, None]
        & ((row_index // R - east_base)[:, None] == depth_range)
    ).astype(jnp.float32)
    south_pick = ((col_index < W_MAX)[:, None] & ((col_index // R)[:, None] == depth_range)).astype(
        jnp.float32
    )
    north_pick = (
        (col_index >= total_y - W_MAX)[:, None]
        & ((col_index // R - north_base)[:, None] == depth_range)
    ).astype(jnp.float32)
    col_reach = (reach_range[:, None] == (col_index // R)[None, :]).astype(jnp.float32)
    row_reach = (reach_range[:, None] == (row_index // R)[None, :]).astype(jnp.float32)
    across = jnp.einsum("eflab,bj->eflaj", own_pieces[0:2], col_reach, precision=PRECISE)
    from_x = jnp.einsum("ia,flaj->flij", west_pick, across[0], precision=PRECISE) + jnp.einsum(
        "ia,flaj->flij", east_pick, across[1], precision=PRECISE
    )
    along_y = jnp.einsum("eflab,bi->eflai", own_pieces[2:4], row_reach, precision=PRECISE)
    from_y = jnp.einsum("ja,flai->flij", south_pick, along_y[0], precision=PRECISE) + jnp.einsum(
        "ja,flai->flij", north_pick, along_y[1], precision=PRECISE
    )
    in_x = (row_index < W_MAX) | (row_index >= total_x - W_MAX)
    target = jnp.where(in_x[:, None], from_x, from_y)
    weight = edge_weight(zone_width, row_index, col_index, total_x, total_y)
    weight = jnp.where(active, weight, 0.0)
    return relaxed_in + weight * (target - relaxed_in)


def local(state, metric, placement, zones):
    fields = state[0]
    terrain = metric[0]
    levels, size_x, size_y = (fields.shape[1], fields.shape[2], fields.shape[3])
    total_x = size_x * lax.axis_size("gx")
    total_y = size_y * lax.axis_size("gy")
    nest_count = placement.shape[0]
    group_index = lax.axis_index("nest")
    row_start = lax.axis_index("gx") * size_x
    col_start = lax.axis_index("gy") * size_y
    foot_x = (total_x + R - 1) // R
    foot_y = (total_y + R - 1) // R
    span_len = 64 * ((max(foot_x, foot_y) + 63) // 64)
    own_group = jnp.minimum(group_index, nest_count - 1)
    start_three = jnp.stack([fields[0], fields[1], fields[3]])
    pieces = boundary_pieces(
        start_three, placement, row_start, col_start, total_x, total_y, foot_x, foot_y, span_len
    )
    summed = lax.psum(pieces, ("gx", "gy"))
    arrived = broadcast(summed, "nest", nest_count)
    own_pieces = arrived[own_group]
    sigma_col = (1.0 - (jnp.arange(levels, dtype=jnp.float32) + 0.5) / levels)[:, None, None]
    current = (fields[0], fields[1], fields[2], fields[3])
    for substep in range(SUB):
        current = step_each(current, terrain, sigma_col)
    active = group_index < nest_count
    moved_three = jnp.stack([current[0], current[1], current[3]])
    relaxed = relax_edges(
        moved_three, own_pieces, zones[own_group], row_start, col_start, total_x, total_y, active
    )
    result = jnp.stack([relaxed[0], relaxed[1], current[2], relaxed[2]])
    return result[None]


def solution(mesh):
    return jax.shard_map(
        local,
        mesh=mesh,
        in_specs=(P("nest", None, None, "gx", "gy"), P("nest", None, "gx", "gy"), P(), P()),
        out_specs=P("nest", None, None, "gx", "gy"),
        check_vma=False,
    )
```

profile of v0, /device:TPU:1, one launch (start us, length us, event | category | flops | bytes accessed | tf_op | source)
XLA Modules:
  0.0 865.6 jit_solution(14164995903394578647)
XLA Ops:
  6.5 0.9 slice_bitcast_fusion.2
  7.5 0.8 add_bitcast_fusion.1
  8.7 1.0 fusion.21
  10.1 0.8 fusion.10
  10.9 1.0 fusion
  11.9 1.9 pad_maximum_fusion
  13.9 4.2 collective-permute-start.1
  18.1 1.3 collective-permute-start
  20.3 1.4 divide_maximum_fusion
  21.6 1.3 maximum_maximum_fusion
  23.2 5.4 collective-permute-start.3
  28.5 2.5 collective-permute-start.2
  31.2 3.3 collective-permute-done.2
  34.7 1.3 collective-permute-start.4
  36.0 4.4 collective-permute-start.5
  40.4 0.7 collective-permute-done.5
  41.3 2.7 collective-permute-start.7
  44.0 1.9 collective-permute-start.6
  45.9 0.8 collective-permute-done.7
  46.7 5.1 collective-permute-done.6
  52.0 3.6 collective-permute-start.9
  55.7 1.3 collective-permute-start.8
  57.0 5.0 collective-permute-done.8
  62.1 2.5 collective-permute-start.11
  64.6 1.9 collective-permute-start.10
  66.7 3.9 collective-permute-done.10
  70.8 1.3 collective-permute-start.12
  72.1 5.1 collective-permute-start.13
  77.2 0.8 collective-permute-done.13
  78.1 2.7 collective-permute-start.15
  80.8 1.9 collective-permute-start.14
  82.7 0.7 collective-permute-done.15
  83.4 4.7 collective-permute-done.14
  88.3 6.4 collective-permute-start.17
  94.7 1.3 collective-permute-start.16
  96.0 3.9 collective-permute-done.16
  100.1 2.1 collective-permute-start.19
  102.2 2.2 collective-permute-start.18
  104.5 4.1 collective-permute-done.18
  108.8 1.3 collective-permute-start.20
  110.1 4.9 collective-permute-start.21
  115.1 0.7 collective-permute-done.21
  115.9 2.7 collective-permute-start.23
  118.6 1.9 collective-permute-start.22
  120.5 0.9 collective-permute-done.23
  121.5 6.1 collective-permute-done.22
  127.8 4.3 collective-permute-start.25
  132.1 1.3 collective-permute-start.24
  133.5 438.1 %all-reduce.3.cloned.1.call-done = f32[7,4,3,8,3,384]{5,3,4,2,1,0:T(8,128)} async-done(((f32[7,4,3,8,3,384]{5,3,4,2,1,0:T(8,128)}), f32[7,4,3,8,3,384]{5,3,4,2,1,0:T(8,128)}) %all-reduce.3.cloned.1.call-update) | async-done | bytes 3096592 | tf_op jit(solution)/shard_map/psum | solution.py:153
  571.6 1.9 broadcast_select_fusion
  573.7 1.9 collective-permute-start.27
  575.6 3.8 collective-permute-start.26
  579.4 2.1 collective-permute-done.26
  581.7 1.3 collective-permute-start.28
  583.0 4.0 collective-permute-start.29
  587.1 0.7 collective-permute-done.29
  588.0 3.0 collective-permute-start.31
  590.9 1.9 collective-permute-start.30
  592.9 5.6 collective-permute-done.31
  598.5 62.3 %collective-permute-done.30 = f32[2,8,18,1]{3,2,1,0:T(8,128)S(1)} collective-permute-done((f32[2,8,18,1]{3,2,1,0:T(8,128)S(1)}, f32[2,8,18,1]{3,2,1,0:T(8,128)S(1)}, u32[]{:S(2)}, u32[]{:S(2)}) %collective-permute-start.30) | collective-permute-done | bytes 1184 | tf_op jit(solution)/shard_map/ppermute | solution.py:23
  661.1 193.1 %all-reduce.5.cloned.1.call-done = f32[7,4,3,8,3,384]{5,3,4,2,1,0:T(8,128)} async-done(((f32[7,4,3,8,3,384]{5,3,4,2,1,0:T(8,128)}), f32[7,4,3,8,3,384]{5,3,4,2,1,0:T(8,128)}) %all-reduce.5.cloned.1.call-update) | async-done | bytes 3096592 | tf_op jit(solution)/shard_map/psum | solution.py:30
  854.2 1.2 fusion.15
  855.4 1.2 fusion.16
  858.1 0.7 maximum_bitcast_fusion
  (127 shorter events, 6.3 us)
Async XLA Ops:
  6.5 565.0 %all-reduce.3.cloned.1.call-start = ((), (), s32[]{:S(2)}) async-start(), calls=%async_computation | async-start | bytes 6193152 | tf_op jit(solution)/shard_map/psum | solution.py:153
  13.8 5.7 copy-start
  13.8 5.7 copy-start.1
  13.8 5.8 copy-start.2
  13.8 840.3 %all-reduce.5.cloned.1.call-start = ((), (), s32[]{:S(2)}) async-start(), calls=%async_computation.1 | async-start | bytes 6193152 | tf_op jit(solution)/shard_map/psum | solution.py:30
  13.9 9.1 %collective-permute-start.1 = (f32[8,1,128]{2,1,0:T(1,128)S(1)}, f32[8,1,128]{2,1,0:T(1,128)S(1)}, u32[]{:S(2)}, u32[]{:S(2)}) collective-permute-start(f32[8,1,128]{2,1,0:T(1,128)S(1)} %get-tuple-element.182), channel_id=1, source_target_pairs={{0,8},{8,16},{16,24},{24,32},{32,40},{40,48},{48,56},{1,9},{9,17},... | collective-permute-start | bytes 12296 | tf_op jit(solution)/shard_map/ppermute | solution.py:22
  18.1 5.0 collective-permute-start
  23.2 8.0 collective-permute-start.3
  28.5 5.9 collective-permute-start.2
  34.7 5.7 collective-permute-start.4
  36.0 5.2 collective-permute-start.5
  41.3 5.5 collective-permute-start.7
  44.0 7.8 collective-permute-start.6
  52.0 5.0 collective-permute-start.9
  55.7 6.3 collective-permute-start.8
  62.1 4.6 collective-permute-start.11
  64.6 5.9 collective-permute-start.10
  70.8 6.4 collective-permute-start.12
  72.1 5.8 collective-permute-start.13
  78.1 5.3 collective-permute-start.15
  80.8 7.3 collective-permute-start.14
  88.3 7.7 collective-permute-start.17
  94.7 5.2 collective-permute-start.16
  100.1 4.5 collective-permute-start.19
  102.2 6.4 collective-permute-start.18
  108.8 6.3 collective-permute-start.20
  110.1 5.7 collective-permute-start.21
  115.9 5.5 collective-permute-start.23
  118.6 9.0 %collective-permute-start.22 = (f32[2,8,18,1]{3,2,1,0:T(8,128)S(1)}, f32[2,8,18,1]{3,2,1,0:T(8,128)S(1)}, u32[]{:S(2)}, u32[]{:S(2)}) collective-permute-start(f32[2,8,18,1]{3,2,1,0:T(8,128)S(1)} %get-tuple-element.35), channel_id=1, source_target_pairs={{1,0},{2,1},{3,2},{4,3},{5,4},{6,5},{7,6},{9,8},{10,9},{11,10},{12... | collective-permute-start | bytes 3464 | tf_op jit(solution)/shard_map/ppermute | solution.py:23
  127.8 445.8 %collective-permute-start.25 = (f32[8,1,128]{2,1,0:T(1,128)S(1)}, f32[8,1,128]{2,1,0:T(1,128)S(1)}, u32[]{:S(2)}, u32[]{:S(2)}) collective-permute-start(f32[8,1,128]{2,1,0:T(1,128)S(1)} %get-tuple-element.171), channel_id=1, source_target_pairs={{0,8},{8,16},{16,24},{24,32},{32,40},{40,48},{48,56},{1,9},{9,17},... | collective-permute-start | bytes 12296 | tf_op jit(solution)/shard_map/ppermute | solution.py:22
  132.1 441.5 %collective-permute-start.24 = (f32[8,1,128]{2,1,0:T(1,128)S(1)}, f32[8,1,128]{2,1,0:T(1,128)S(1)}, u32[]{:S(2)}, u32[]{:S(2)}) collective-permute-start(f32[8,1,128]{2,1,0:T(1,128)S(1)} %get-tuple-element.172), channel_id=1, source_target_pairs={{8,0},{16,8},{24,16},{32,24},{40,32},{48,40},{56,48},{9,1},{17,9},... | collective-permute-start | bytes 12296 | tf_op jit(solution)/shard_map/ppermute | solution.py:23
  573.7 5.7 collective-permute-start.27
  575.6 5.9 collective-permute-start.26
  581.7 5.3 collective-permute-start.28
  583.0 4.8 collective-permute-start.29
  588.0 10.5 %collective-permute-start.31 = (f32[2,8,18,1]{3,2,1,0:T(8,128)S(1)}, f32[2,8,18,1]{3,2,1,0:T(8,128)S(1)}, u32[]{:S(2)}, u32[]{:S(2)}) collective-permute-start(f32[2,8,18,1]{3,2,1,0:T(8,128)S(1)} %get-tuple-element.34), channel_id=1, source_target_pairs={{0,1},{1,2},{2,3},{3,4},{4,5},{5,6},{6,7},{8,9},{9,10},{10,11},{11... | collective-permute-start | bytes 3464 | tf_op jit(solution)/shard_map/ppermute | solution.py:22
  590.9 69.9 %collective-permute-start.30 = (f32[2,8,18,1]{3,2,1,0:T(8,128)S(1)}, f32[2,8,18,1]{3,2,1,0:T(8,128)S(1)}, u32[]{:S(2)}, u32[]{:S(2)}) collective-permute-start(f32[2,8,18,1]{3,2,1,0:T(8,128)S(1)} %get-tuple-element.33), channel_id=1, source_target_pairs={{1,0},{2,1},{3,2},{4,3},{5,4},{6,5},{7,6},{9,8},{10,9},{11,10},{12... | collective-permute-start | bytes 3464 | tf_op jit(solution)/shard_map/ppermute | solution.py:23
Sparse Core Ops, SparseCore 0:
  14.0 557.5 all-reduce.2
  574.5 279.5 all-reduce.4
where the time goes:
time: 867 us; the launch traced here: 866 us
  waiting for transfers between devices  743 us (86%)
  starting transfers between devices  88.2 us (10%)
  between operations  14.5 us (2%)
  other arithmetic  10.4 us (1%)
    psum x1, waiting for transfers between devices, local(): summed = lax.psum(pieces, ('gx', 'gy'))  438 us
    psum x1, waiting for transfers between devices, broadcast(): return lax.psum(block, axis)  193 us
    ppermute x16, waiting for transfers between devices, extended(): after = lax.ppermute(initial, axis, down)  100 us
    ppermute x16, starting transfers between devices, extended(): before = lax.ppermute(last, axis, up)  59.8 us
    ppermute x16, starting transfers between devices, extended(): after = lax.ppermute(initial, axis, down)  28.4 us
  transfers between devices with their start and end apart: 34, of which 20 were waited for; matrix products, arithmetic and copies ran while one was open for 1% of the time, Pallas kernels for 0%

commit v1 on v0

--- a/solution.py
+++ b/solution.py
@@ -27,7 +27,7 @@
 
 def broadcast(block, axis, owner):
     block = jnp.where(lax.axis_index(axis) == owner, block, jnp.zeros_like(block))
-    return lax.psum(block, axis)
+    return jnp.sum(lax.all_gather(block, axis), axis=0)
 
 
 def vertical(field):

time: 867 us -> 1050 us (1.21)
  waiting for transfers between devices: 743 us -> 915 us
    all_gather x0 -> x1, waiting for transfers between devices: none -> 221 us  [broadcast(): return jnp.sum(lax.all_gather(block, axis), axis=0)]
    psum x1 -> x0, waiting for transfers between devices: 193 us -> none  [broadcast(): return lax.psum(block, axis)]
    psum x1, waiting for transfers between devices: 438 us -> 557 us  [local(): summed = lax.psum(pieces, ('gx', 'gy'))]
    ppermute x16, waiting for transfers between devices: 11 us -> 30.3 us  [extended(): before = lax.ppermute(last, axis, up)]
  transfers between devices with their start and end apart: 34 -> 34, of which waited for: 20 -> 23; matrix products, arithmetic and copies ran while one was open for 1% -> 1% of each run, Pallas kernels for 0% -> 0%
where the time goes in v1:
time: 1050 us; the launch traced here: 1040 us
  waiting for transfers between devices  915 us (87%)
  starting transfers between devices  87 us (8%)
  other arithmetic  19.6 us (2%)
  between operations  14.5 us (1%)
    psum x1, waiting for transfers between devices, local(): summed = lax.psum(pieces, ('gx', 'gy'))  557 us
    all_gather x1, waiting for transfers between devices, broadcast(): return jnp.sum(lax.all_gather(block, axis), axis=0)  221 us
    ppermute x16, waiting for transfers between devices, extended(): after = lax.ppermute(initial, axis, down)  106 us
    ppermute x16, starting transfers between devices, extended(): before = lax.ppermute(last, axis, up)  57 us
    ppermute x16, waiting for transfers between devices, extended(): before = lax.ppermute(last, axis, up)  30.3 us
    ppermute x16, starting transfers between devices, extended(): after = lax.ppermute(initial, axis, down)  30 us
  transfers between devices with their start and end apart: 34, of which 23 were waited for; matrix products, arithmetic and copies ran while one was open for 1% of the time, Pallas kernels for 0%

profile of v1, /device:TPU:1, one launch (start us, length us, event | category | flops | bytes accessed | tf_op | source)
XLA Modules:
  0.0 1044.3 jit_solution(14581259869398359712)
XLA Ops:
  6.5 0.9 slice_bitcast_fusion.2
  7.5 0.8 add_bitcast_fusion.1
  8.7 1.0 fusion.21
  10.1 0.8 fusion.10
  10.9 1.0 fusion
  11.9 1.9 pad_maximum_fusion
  13.9 557.2 %all-reduce.2.cloned.1.call-done = f32[7,4,3,8,3,384]{5,3,4,2,1,0:T(8,128)} async-done(((f32[7,4,3,8,3,384]{5,3,4,2,1,0:T(8,128)}), f32[7,4,3,8,3,384]{5,3,4,2,1,0:T(8,128)}) %all-reduce.2.cloned.1.call-update) | async-done | bytes 3096592 | tf_op jit(solution)/shard_map/psum | solution.py:153
  571.1 1.8 broadcast_select_fusion
  573.0 1.4 collective-permute-start.1
  574.4 1.3 collective-permute-start
  576.5 1.3 maximum_maximum_fusion
  577.8 1.2 divide_maximum_fusion
  579.4 1.9 collective-permute-start.3
  581.3 4.4 collective-permute-start.2
  585.9 1.4 collective-permute-done.2
  587.4 1.3 collective-permute-start.4
  588.7 4.6 collective-permute-start.5
  593.4 0.7 collective-permute-done.5
  594.3 2.7 collective-permute-start.7
  596.9 1.9 collective-permute-start.6
  598.9 7.5 collective-permute-done.7
  606.4 8.6 collective-permute-done.6
  615.2 4.7 collective-permute-start.9
  619.9 1.3 collective-permute-start.8
  621.2 5.3 collective-permute-done.8
  626.6 1.9 collective-permute-start.11
  628.6 2.4 collective-permute-start.10
  631.1 1.4 collective-permute-done.11
  632.5 15.6 %collective-permute-done.10 = f32[8,18,1]{2,1,0:T(8,128)S(1)} collective-permute-done((f32[8,18,1]{2,1,0:T(8,128)S(1)}, f32[8,18,1]{2,1,0:T(8,128)S(1)}, u32[]{:S(2)}, u32[]{:S(2)}) %collective-permute-start.10) | collective-permute-done | bytes 608 | tf_op jit(solution)/shard_map/ppermute | solution.py:23
  648.4 1.3 collective-permute-start.12
  649.7 12.7 %collective-permute-start.13 = (f32[2,8,1,128]{3,2,1,0:T(1,128)S(1)}, f32[2,8,1,128]{3,2,1,0:T(1,128)S(1)}, u32[]{:S(2)}, u32[]{:S(2)}) collective-permute-start(f32[2,8,1,128]{3,2,1,0:T(1,128)S(1)} %get-tuple-element.47), channel_id=1, source_target_pairs={{0,8},{8,16},{16,24},{24,32},{32,40},{40,48},{48,56},{1,9},{9,17},... | collective-permute-start | bytes 24584 | tf_op jit(solution)/shard_map/ppermute | solution.py:22
  663.3 1.9 collective-permute-start.15
  665.2 2.4 collective-permute-start.14
  667.7 4.5 collective-permute-done.15
  672.1 8.9 collective-permute-done.14
  681.2 4.0 collective-permute-start.17
  685.3 1.3 collective-permute-start.16
  686.6 3.0 collective-permute-done.16
  689.7 2.8 collective-permute-start.19
  692.5 1.9 collective-permute-start.18
  694.6 3.9 collective-permute-done.18
  698.6 1.3 collective-permute-start.20
  699.9 4.0 collective-permute-start.21
  704.8 3.0 collective-permute-start.23
  707.8 1.9 collective-permute-start.22
  709.7 6.6 collective-permute-done.23
  716.4 6.4 collective-permute-done.22
  723.0 3.4 collective-permute-start.25
  726.4 1.3 collective-permute-start.24
  727.8 4.0 collective-permute-done.24
  731.9 1.9 collective-permute-start.27
  733.8 2.4 collective-permute-start.26
  736.2 2.1 collective-permute-done.27
  738.4 30.2 %collective-permute-done.26 = f32[8,18,1]{2,1,0:T(8,128)S(1)} collective-permute-done((f32[8,18,1]{2,1,0:T(8,128)S(1)}, f32[8,18,1]{2,1,0:T(8,128)S(1)}, u32[]{:S(2)}, u32[]{:S(2)}) %collective-permute-start.26) | collective-permute-done | bytes 608 | tf_op jit(solution)/shard_map/ppermute | solution.py:23
  768.7 1.3 collective-permute-start.28
  770.0 4.0 collective-permute-start.29
  774.1 0.7 collective-permute-done.29
  775.0 2.1 collective-permute-start.31
  777.1 2.2 collective-permute-start.30
  779.3 5.3 collective-permute-done.31
  784.6 19.2 %collective-permute-done.30 = f32[2,8,18,1]{3,2,1,0:T(8,128)S(1)} collective-permute-done((f32[2,8,18,1]{3,2,1,0:T(8,128)S(1)}, f32[2,8,18,1]{3,2,1,0:T(8,128)S(1)}, u32[]{:S(2)}, u32[]{:S(2)}) %collective-permute-start.30) | collective-permute-done | bytes 1184 | tf_op jit(solution)/shard_map/ppermute | solution.py:23
  804.1 221.3 %all-gather.3.cloned.1.call-done = f32[56,4,3,8,3,384]{5,3,4,2,1,0:T(8,128)} async-done(((f32[7,4,3,8,3,384]{5,3,4,2,1,0:T(8,128)}), f32[56,4,3,8,3,384]{5,3,4,2,1,0:T(8,128)}) %all-gather.3.cloned.1.call-update) | async-done | bytes 24772624 | tf_op jit(solution)/shard_map/all_gather | solution.py:30
  1025.4 9.3 reduce_sum.9
  1036.7 0.7 maximum_bitcast_fusion
  (128 shorter events, 8.3 us)
Async XLA Ops:
  6.5 564.5 %all-reduce.2.cloned.1.call-start = ((), (), s32[]{:S(2)}) async-start(), calls=%async_computation | async-start | bytes 6193152 | tf_op jit(solution)/shard_map/psum | solution.py:153
  13.8 1011.6 %all-gather.3.cloned.1.call-start = ((), (), s32[]{:S(2)}) async-start(), calls=%async_computation.1 | async-start | bytes 27869184 | tf_op jit(solution)/shard_map/all_gather | solution.py:30
  572.9 2.9 copy-start.2
  572.9 6.2 copy-start
  572.9 6.2 copy-start.1
  573.0 6.2 collective-permute-start.1
  574.4 4.8 collective-permute-start
  579.4 6.5 collective-permute-start.3
  581.3 5.9 collective-permute-start.2
  587.4 6.0 collective-permute-start.4
  588.7 5.4 collective-permute-start.5
  594.3 12.1 %collective-permute-start.7 = (f32[2,8,18,1]{3,2,1,0:T(8,128)S(1)}, f32[2,8,18,1]{3,2,1,0:T(8,128)S(1)}, u32[]{:S(2)}, u32[]{:S(2)}) collective-permute-start(f32[2,8,18,1]{3,2,1,0:T(8,128)S(1)} %get-tuple-element.40), channel_id=1, source_target_pairs={{0,1},{1,2},{2,3},{3,4},{4,5},{5,6},{6,7},{8,9},{9,10},{10,11},{11... | collective-permute-start | bytes 3464 | tf_op jit(solution)/shard_map/ppermute | solution.py:22
  596.9 18.1 %collective-permute-start.6 = (f32[2,8,18,1]{3,2,1,0:T(8,128)S(1)}, f32[2,8,18,1]{3,2,1,0:T(8,128)S(1)}, u32[]{:S(2)}, u32[]{:S(2)}) collective-permute-start(f32[2,8,18,1]{3,2,1,0:T(8,128)S(1)} %get-tuple-element.39), channel_id=1, source_target_pairs={{1,0},{2,1},{3,2},{4,3},{5,4},{6,5},{7,6},{9,8},{10,9},{11,10},{12... | collective-permute-start | bytes 3464 | tf_op jit(solution)/shard_map/ppermute | solution.py:23
  615.2 6.0 collective-permute-start.9
  619.9 6.6 collective-permute-start.8
  626.6 5.9 collective-permute-start.11
  628.6 19.6 %collective-permute-start.10 = (f32[8,18,1]{2,1,0:T(8,128)S(1)}, f32[8,18,1]{2,1,0:T(8,128)S(1)}, u32[]{:S(2)}, u32[]{:S(2)}) collective-permute-start(f32[8,18,1]{2,1,0:T(8,128)S(1)} %get-tuple-element.55), channel_id=1, source_target_pairs={{1,0},{2,1},{3,2},{4,3},{5,4},{6,5},{7,6},{9,8},{10,9},{11,10},{12... | collective-permute-start | bytes 1736 | tf_op jit(solution)/shard_map/ppermute | solution.py:23
  648.4 14.1 %collective-permute-start.12 = (f32[2,8,1,128]{3,2,1,0:T(1,128)S(1)}, f32[2,8,1,128]{3,2,1,0:T(1,128)S(1)}, u32[]{:S(2)}, u32[]{:S(2)}) collective-permute-start(f32[2,8,1,128]{3,2,1,0:T(1,128)S(1)} %get-tuple-element.48), channel_id=1, source_target_pairs={{8,0},{16,8},{24,16},{32,24},{40,32},{48,40},{56,48},{9,1},{17,9},... | collective-permute-start | bytes 24584 | tf_op jit(solution)/shard_map/ppermute | solution.py:23
  649.7 13.5 %collective-permute-start.13 = (f32[2,8,1,128]{3,2,1,0:T(1,128)S(1)}, f32[2,8,1,128]{3,2,1,0:T(1,128)S(1)}, u32[]{:S(2)}, u32[]{:S(2)}) collective-permute-start(f32[2,8,1,128]{3,2,1,0:T(1,128)S(1)} %get-tuple-element.47), channel_id=1, source_target_pairs={{0,8},{8,16},{16,24},{24,32},{32,40},{40,48},{48,56},{1,9},{9,17},... | collective-permute-start | bytes 24584 | tf_op jit(solution)/shard_map/ppermute | solution.py:22
  663.3 8.8 collective-permute-start.15
  665.2 15.8 %collective-permute-start.14 = (f32[2,8,18,1]{3,2,1,0:T(8,128)S(1)}, f32[2,8,18,1]{3,2,1,0:T(8,128)S(1)}, u32[]{:S(2)}, u32[]{:S(2)}) collective-permute-start(f32[2,8,18,1]{3,2,1,0:T(8,128)S(1)} %get-tuple-element.37), channel_id=1, source_target_pairs={{1,0},{2,1},{3,2},{4,3},{5,4},{6,5},{7,6},{9,8},{10,9},{11,10},{12... | collective-permute-start | bytes 3464 | tf_op jit(solution)/shard_map/ppermute | solution.py:23
  681.2 5.4 collective-permute-start.17
  685.3 4.4 collective-permute-start.16
  689.7 4.8 collective-permute-start.19
  692.5 5.9 collective-permute-start.18
  698.6 5.4 collective-permute-start.20
  699.9 4.8 collective-permute-start.21
  704.8 11.5 %collective-permute-start.23 = (f32[2,8,18,1]{3,2,1,0:T(8,128)S(1)}, f32[2,8,18,1]{3,2,1,0:T(8,128)S(1)}, u32[]{:S(2)}, u32[]{:S(2)}) collective-permute-start(f32[2,8,18,1]{3,2,1,0:T(8,128)S(1)} %get-tuple-element.36), channel_id=1, source_target_pairs={{0,1},{1,2},{2,3},{3,4},{4,5},{5,6},{6,7},{8,9},{9,10},{10,11},{11... | collective-permute-start | bytes 3464 | tf_op jit(solution)/shard_map/ppermute | solution.py:22
  707.8 15.0 %collective-permute-start.22 = (f32[2,8,18,1]{3,2,1,0:T(8,128)S(1)}, f32[2,8,18,1]{3,2,1,0:T(8,128)S(1)}, u32[]{:S(2)}, u32[]{:S(2)}) collective-permute-start(f32[2,8,18,1]{3,2,1,0:T(8,128)S(1)} %get-tuple-element.35), channel_id=1, source_target_pairs={{1,0},{2,1},{3,2},{4,3},{5,4},{6,5},{7,6},{9,8},{10,9},{11,10},{12... | collective-permute-start | bytes 3464 | tf_op jit(solution)/shard_map/ppermute | solution.py:23
  723.0 4.8 collective-permute-start.25
  726.4 5.4 collective-permute-start.24
  731.9 6.5 collective-permute-start.27
  733.8 34.7 %collective-permute-start.26 = (f32[8,18,1]{2,1,0:T(8,128)S(1)}, f32[8,18,1]{2,1,0:T(8,128)S(1)}, u32[]{:S(2)}, u32[]{:S(2)}) collective-permute-start(f32[8,18,1]{2,1,0:T(8,128)S(1)} %get-tuple-element.51), channel_id=1, source_target_pairs={{1,0},{2,1},{3,2},{4,3},{5,4},{6,5},{7,6},{9,8},{10,9},{11,10},{12... | collective-permute-start | bytes 1736 | tf_op jit(solution)/shard_map/ppermute | solution.py:23
  768.7 5.4 collective-permute-start.28
  770.0 4.8 collective-permute-start.29
  775.0 9.7 collective-permute-start.31
  777.1 26.7 %collective-permute-start.30 = (f32[2,8,18,1]{3,2,1,0:T(8,128)S(1)}, f32[2,8,18,1]{3,2,1,0:T(8,128)S(1)}, u32[]{:S(2)}, u32[]{:S(2)}) collective-permute-start(f32[2,8,18,1]{3,2,1,0:T(8,128)S(1)} %get-tuple-element.33), channel_id=1, source_target_pairs={{1,0},{2,1},{3,2},{4,3},{5,4},{6,5},{7,6},{9,8},{10,9},{11,10},{12... | collective-permute-start | bytes 3464 | tf_op jit(solution)/shard_map/ppermute | solution.py:23
Sparse Core Ops, SparseCore 0:
  14.0 557.0 all-reduce.1
  574.3 451.0 all-gather.2
